TPU v7x, 32 devices: a whole 2x2x4 slice. The times are simulated.
32 devices in a mesh: expert: 8 (over z, x), shard: 4 (over y, core).
Axes of the slice: x: 2, y: 2, z: 4, core: 2. Of those that a mesh axis runs over, the one named last changes fastest.
Arguments:
- tokens: bfloat16 [25216, 512], P(('expert', 'shard')), may hold values from -6 to 6
- teacher: bfloat16 [25216, 512], P(('expert', 'shard')), may hold values from -6 to 6
- valid_mask: int32 [25216], P(('expert', 'shard')), may hold values from 0 to 1, as said below
- routes: int32 [25216, 2], P(('expert', 'shard')), may hold values from 0 to 7, all different within a row; in each aligned block of 788 rows (0 to 787, 788 to 1575, ...) at most 394 rows name the same one
- mixer_weight: bfloat16 [512, 1536], P('shard'), may hold values from -0.25 to 0.25
- merge_weight: bfloat16 [512, 512], P('shard'), may hold values from -1 to 1
- router_weight: bfloat16 [512, 8], P('shard'), may hold values from -0.1875 to 0.1875
- norm_gain: bfloat16 [2, 512], P(None, 'shard'), may hold values from 0.5 to 1.5
- norm_shift: bfloat16 [2, 512], P(None, 'shard'), may hold values from -0.59765625 to 0.59765625
- up_weight: bfloat16 [8, 512, 2048], P('expert', None, 'shard'), may hold values from -0.25 to 0.25
- inner_bias: bfloat16 [8, 2048], P('expert', 'shard'), may hold values from -0.59765625 to 0.59765625
- down_weight: bfloat16 [8, 2048, 512], P('expert', 'shard'), may hold values from -0.75 to 0.75
- outer_bias: bfloat16 [8, 512], P('expert', 'shard'), may hold values from -6 to 6
Outputs:
- output: bfloat16 [25216, 512], P(('expert', 'shard'))
- loss_value: float32 [], replicated
- token_grad: float32 [25216, 512], P(('expert', 'shard'))
- mixer_grad: float32 [512, 1536], P('shard')
- merge_grad: float32 [512, 512], P('shard')
- router_grad: float32 [512, 8], P('shard')
- gain_grad: float32 [2, 512], P(None, 'shard')
- shift_grad: float32 [2, 512], P(None, 'shard')
- up_grad: float32 [8, 512, 2048], P('expert', None, 'shard')
- inner_grad: float32 [8, 2048], P('expert', 'shard')
- down_grad: float32 [8, 2048, 512], P('expert', 'shard')
- outer_grad: float32 [8, 512], P('expert', 'shard')
Inputs may be any that keep to these rules, and one draw needn't show every extreme that they name: `routes`: each token names two different experts. Among the 2 x 788 choices of the tokens of one device no expert is named more than 394 times, a bound that some block reaches. `valid_mask`: the first of each device's 788 tokens is valid.
All inputs are finite; a program needn't handle non-finite values.
Results may differ from a plain program's by a relative error of at most 0.011.
Values may be sent and summed in bfloat16 or wider, within the bound.
No kernel may reach another device: no remote copies, remote signals or barrier semaphores. Data moves between devices by JAX's collectives and lax.ppermute only.
A program may use at most 192 MiB of HBM per device.

v0:
```python
import jax
import jax.numpy as jnp
from jax import lax
from jax.sharding import PartitionSpec as P

HEADS = 8
HEAD_DIM = 64
SEQ = 197
norm_eps = 1e-06


def layer_norm(inputs, scale_row, shift_row):
    centered = inputs - jnp.mean(inputs, axis=-1, keepdims=True)
    variance = jnp.mean(centered * centered, axis=-1, keepdims=True)
    return centered * lax.rsqrt(variance + norm_eps) * scale_row + shift_row


def gelu_tanh(values):
    return jax.nn.gelu(values, approximate=True)


def group_sources(arrays):
    count_src = arrays.shape[0]
    group_size = 8
    return arrays.reshape((count_src // group_size, group_size) + arrays.shape[1:])


def per_device(
    tokens,
    teacher,
    valid_mask,
    routes,
    mixer_weight,
    merge_weight,
    router_weight,
    norm_gain,
    norm_shift,
    up_weight,
    inner_bias,
    down_weight,
    outer_bias,
):
    expert_ways = lax.axis_size("expert")
    shard_ways = lax.axis_size("shard")
    token_count = tokens.shape[0]
    model_width = tokens.shape[1]
    images = token_count // SEQ
    experts = router_weight.shape[1]
    local_experts = up_weight.shape[0]
    capacity = max(2, 4 * token_count // experts)
    scaling = HEAD_DIM ** (-0.5)
    (
        mixer_full,
        merge_full,
        router_full,
        gain_full,
        shift_full,
        up_full,
        inner_full,
        down_full,
        outer_full,
    ) = (
        lax.all_gather(mixer_weight, "shard", axis=0, tiled=True),
        lax.all_gather(merge_weight, "shard", axis=0, tiled=True),
        lax.all_gather(router_weight, "shard", axis=0, tiled=True),
        lax.all_gather(norm_gain, "shard", axis=1, tiled=True),
        lax.all_gather(norm_shift, "shard", axis=1, tiled=True),
        lax.all_gather(up_weight, "shard", axis=2, tiled=True),
        lax.all_gather(inner_bias, "shard", axis=1, tiled=True),
        lax.all_gather(down_weight, "shard", axis=1, tiled=True),
        lax.all_gather(outer_bias, "shard", axis=1, tiled=True),
    )
    gain_rows = gain_full.astype(jnp.float32)
    shift_rows = shift_full.astype(jnp.float32)
    inner_rows = inner_full.astype(jnp.float32)
    outer_rows = outer_full.astype(jnp.float32)
    token_rows = tokens.astype(jnp.float32)
    normed_wide, norm_one_back = jax.vjp(layer_norm, token_rows, gain_rows[0], shift_rows[0])
    normed = normed_wide.astype(jnp.bfloat16)
    mixed_rows = jnp.dot(normed, mixer_full, preferred_element_type=jnp.float32).astype(
        jnp.bfloat16
    )
    shaped = mixed_rows.reshape(images, SEQ, 3, HEADS, HEAD_DIM)
    queries = shaped[:, :, 0]
    key_rows = shaped[:, :, 1]
    value_rows = shaped[:, :, 2]
    scores = (
        jnp.einsum("bqhd,bkhd->bhqk", queries, key_rows, preferred_element_type=jnp.float32)
        * scaling
    )
    top_score = jnp.max(scores, axis=-1, keepdims=True)
    log_total = top_score + jnp.log(jnp.sum(jnp.exp(scores - top_score), axis=-1, keepdims=True))
    weights_low = jnp.exp(scores - log_total).astype(jnp.bfloat16)
    attended = jnp.einsum(
        "bhqk,bkhd->bqhd", weights_low, value_rows, preferred_element_type=jnp.float32
    )
    attended = attended.reshape(token_count, model_width).astype(jnp.bfloat16)
    residual = token_rows + jnp.dot(attended, merge_full, preferred_element_type=jnp.float32)
    normed_two_wide, norm_two_back = jax.vjp(layer_norm, residual, gain_rows[1], shift_rows[1])
    normed_two = normed_two_wide.astype(jnp.bfloat16)
    logits = jnp.dot(normed_two, router_full, preferred_element_type=jnp.float32)
    route_hot = (routes[:, :, None] == jnp.arange(experts, dtype=jnp.int32)[None, None, :]).astype(
        jnp.float32
    )

    def gate_of_logits(logit_rows):
        return jnp.sum(jax.nn.softmax(logit_rows, axis=-1)[:, None, :] * route_hot, axis=2)

    gate_values, gate_back = jax.vjp(gate_of_logits, logits)
    flat_routes = routes.reshape(-1)
    flat_hot = (flat_routes[:, None] == jnp.arange(experts, dtype=jnp.int32)[None, :]).astype(
        jnp.int32
    )
    earlier = jnp.cumsum(flat_hot, axis=0) - flat_hot
    slot_rows = flat_routes * capacity + jnp.sum(earlier * flat_hot, axis=1)
    send_rows = (
        jnp.zeros((experts * capacity, model_width), jnp.bfloat16)
        .at[slot_rows]
        .set(jnp.repeat(normed_two, 2, axis=0))
    )
    send_rows = send_rows.reshape(expert_ways, local_experts, capacity, model_width)

    def expert_rows(arrived_block):
        hidden = (
            jnp.einsum("sjcd,jdf->sjcf", arrived_block, up_full, preferred_element_type=jnp.float32)
            + inner_rows[None, :, None, :]
        )
        active = gelu_tanh(hidden).astype(jnp.bfloat16)
        produced = (
            jnp.einsum("sjcf,jfd->sjcd", active, down_full, preferred_element_type=jnp.float32)
            + outer_rows[None, :, None, :]
        )
        return produced.astype(jnp.bfloat16)

    arrived_rows = lax.all_to_all(send_rows, "expert", split_axis=0, concat_axis=0, tiled=True)
    produced = lax.map(expert_rows, group_sources(arrived_rows)).reshape(arrived_rows.shape)
    arrived, produced = (arrived_rows, produced)
    returned = lax.all_to_all(produced, "expert", split_axis=0, concat_axis=0, tiled=True)
    picked = (
        returned.reshape(experts * capacity, model_width)[slot_rows]
        .reshape(token_count, 2, model_width)
        .astype(jnp.float32)
    )
    block_out = residual + jnp.sum(gate_values[:, :, None] * picked, axis=1)
    valid_rows = valid_mask.astype(jnp.float32)
    error_rows = block_out - teacher.astype(jnp.float32)
    squared_sum = jnp.sum(valid_rows * jnp.sum(error_rows * error_rows, axis=1))
    total_error, total_count = lax.psum((squared_sum, jnp.sum(valid_rows)), ("expert", "shard"))
    loss_value = total_error / (2.0 * total_count)
    all_tokens = token_count * expert_ways * shard_ways
    final_grad = all_tokens / total_count * valid_rows[:, None] * error_rows
    gate_grad = jnp.sum(final_grad[:, None, :] * picked, axis=2)
    logit_low = gate_back(gate_grad)[0].astype(jnp.bfloat16)
    router_term = jnp.einsum("td,te->de", normed_two, logit_low, preferred_element_type=jnp.float32)
    router_back = jnp.einsum(
        "te,de->td", logit_low, router_full, preferred_element_type=jnp.float32
    )
    sent_grad = (
        (gate_values[:, :, None] * final_grad[:, None, :])
        .astype(jnp.bfloat16)
        .reshape(2 * token_count, model_width)
    )
    grad_send = (
        jnp.zeros((experts * capacity, model_width), jnp.bfloat16).at[slot_rows].set(sent_grad)
    )
    grad_send = grad_send.reshape(expert_ways, local_experts, capacity, model_width)
    grad_arrived = lax.all_to_all(grad_send, "expert", split_axis=0, concat_axis=0, tiled=True)

    def expert_backward(totals, pieces):
        up_total, inner_total, down_total, outer_total = totals
        inputs_block, grads_block = pieces
        hidden = (
            jnp.einsum("sjcd,jdf->sjcf", inputs_block, up_full, preferred_element_type=jnp.float32)
            + inner_rows[None, :, None, :]
        )
        active_wide, gelu_back = jax.vjp(gelu_tanh, hidden)
        active = active_wide.astype(jnp.bfloat16)
        down_total = down_total + jnp.einsum(
            "sjcf,sjcd->jfd", active, grads_block, preferred_element_type=jnp.float32
        )
        outer_total = outer_total + jnp.sum(grads_block.astype(jnp.float32), axis=(0, 2))
        active_grad = jnp.einsum(
            "sjcd,jfd->sjcf", grads_block, down_full, preferred_element_type=jnp.float32
        )
        hidden_grad = gelu_back(active_grad)[0].astype(jnp.bfloat16)
        inner_total = inner_total + jnp.sum(hidden_grad.astype(jnp.float32), axis=(0, 2))
        up_total = up_total + jnp.einsum(
            "sjcd,sjcf->jdf", inputs_block, hidden_grad, preferred_element_type=jnp.float32
        )
        input_grad = jnp.einsum(
            "sjcf,jdf->sjcd", hidden_grad, up_full, preferred_element_type=jnp.float32
        ).astype(jnp.bfloat16)
        return ((up_total, inner_total, down_total, outer_total), input_grad)

    expert_init = (
        jnp.zeros(up_full.shape, jnp.float32),
        jnp.zeros(inner_full.shape, jnp.float32),
        jnp.zeros(down_full.shape, jnp.float32),
        jnp.zeros(outer_full.shape, jnp.float32),
    )
    expert_totals, input_grads = lax.scan(
        expert_backward, expert_init, (group_sources(arrived), group_sources(grad_arrived))
    )
    up_total, inner_total, down_total, outer_total = expert_totals
    grad_back = lax.all_to_all(
        input_grads.reshape(arrived.shape), "expert", split_axis=0, concat_axis=0, tiled=True
    )
    moe_norm_grad = jnp.sum(
        grad_back.reshape(experts * capacity, model_width)[slot_rows]
        .reshape(token_count, 2, model_width)
        .astype(jnp.float32),
        axis=1,
    )
    norm_two_grad = moe_norm_grad + router_back
    residual_ln_grad, gain_two_grad, shift_two_grad = norm_two_back(norm_two_grad)
    residual_grad = final_grad + residual_ln_grad
    residual_low = residual_grad.astype(jnp.bfloat16)
    merge_term = jnp.einsum("tc,td->cd", attended, residual_low, preferred_element_type=jnp.float32)
    attended_grad = jnp.einsum(
        "td,cd->tc", residual_low, merge_full, preferred_element_type=jnp.float32
    ).astype(jnp.bfloat16)
    attended_grad = attended_grad.reshape(images, SEQ, HEADS, HEAD_DIM)
    again_scores = (
        jnp.einsum("bqhd,bkhd->bhqk", queries, key_rows, preferred_element_type=jnp.float32)
        * scaling
    )
    weights_wide = jnp.exp(again_scores - log_total)
    value_grad = jnp.einsum(
        "bhqk,bqhd->bkhd",
        weights_wide.astype(jnp.bfloat16),
        attended_grad,
        preferred_element_type=jnp.float32,
    )
    weight_grad = jnp.einsum(
        "bqhd,bkhd->bhqk", attended_grad, value_rows, preferred_element_type=jnp.float32
    )
    inner_dot = jnp.sum(weights_wide * weight_grad, axis=-1, keepdims=True)
    score_grad = (weights_wide * (weight_grad - inner_dot)).astype(jnp.bfloat16)
    query_grad = (
        jnp.einsum("bhqk,bkhd->bqhd", score_grad, key_rows, preferred_element_type=jnp.float32)
        * scaling
    )
    key_grad = (
        jnp.einsum("bhqk,bqhd->bkhd", score_grad, queries, preferred_element_type=jnp.float32)
        * scaling
    )
    mixed_grad = (
        jnp.stack([query_grad, key_grad, value_grad], axis=2)
        .reshape(token_count, 3 * model_width)
        .astype(jnp.bfloat16)
    )
    mixer_term = jnp.einsum("tc,tm->cm", normed, mixed_grad, preferred_element_type=jnp.float32)
    norm_one_grad = jnp.einsum(
        "tm,cm->tc", mixed_grad, mixer_full, preferred_element_type=jnp.float32
    )
    token_ln_grad, gain_one_grad, shift_one_grad = norm_one_back(norm_one_grad)
    token_grad = residual_grad + token_ln_grad
    gain_term = jnp.stack([gain_one_grad, gain_two_grad], axis=0)
    shift_term = jnp.stack([shift_one_grad, shift_two_grad], axis=0)
    summed = lax.psum(
        (mixer_term, merge_term, router_term, gain_term, shift_term), ("expert", "shard")
    )
    position = lax.axis_index("shard")
    rows_dev = model_width // shard_ways
    mixer_grad = lax.dynamic_slice_in_dim(summed[0], position * rows_dev, rows_dev, 0)
    merge_grad = lax.dynamic_slice_in_dim(summed[1], position * rows_dev, rows_dev, 0)
    router_grad = lax.dynamic_slice_in_dim(summed[2], position * rows_dev, rows_dev, 0)
    gain_grad = lax.dynamic_slice_in_dim(summed[3], position * rows_dev, rows_dev, 1)
    shift_grad = lax.dynamic_slice_in_dim(summed[4], position * rows_dev, rows_dev, 1)
    up_grad, inner_grad, down_grad, outer_grad = (
        lax.psum_scatter(
            up_total.astype(jnp.bfloat16), "shard", scatter_dimension=2, tiled=True
        ).astype(jnp.float32),
        lax.psum_scatter(
            inner_total.astype(jnp.bfloat16), "shard", scatter_dimension=1, tiled=True
        ).astype(jnp.float32),
        lax.psum_scatter(
            down_total.astype(jnp.bfloat16), "shard", scatter_dimension=1, tiled=True
        ).astype(jnp.float32),
        lax.psum_scatter(
            outer_total.astype(jnp.bfloat16), "shard", scatter_dimension=1, tiled=True
        ).astype(jnp.float32),
    )
    return (
        block_out.astype(jnp.bfloat16),
        loss_value,
        token_grad,
        mixer_grad,
        merge_grad,
        router_grad,
        gain_grad,
        shift_grad,
        up_grad,
        inner_grad,
        down_grad,
        outer_grad,
    )


def solution(mesh):
    in_specs = (
        P(("expert", "shard"), None),
        P(("expert", "shard"), None),
        P(("expert", "shard")),
        P(("expert", "shard"), None),
        P("shard", None),
        P("shard", None),
        P("shard", None),
        P(None, "shard"),
        P(None, "shard"),
        P("expert", None, "shard"),
        P("expert", "shard"),
        P("expert", "shard", None),
        P("expert", "shard"),
    )
    out_specs = (
        P(("expert", "shard"), None),
        P(),
        P(("expert", "shard"), None),
        P("shard", None),
        P("shard", None),
        P("shard", None),
        P(None, "shard"),
        P(None, "shard"),
        P("expert", None, "shard"),
        P("expert", "shard"),
        P("expert", "shard", None),
        P("expert", "shard"),
    )
    return jax.shard_map(
        per_device, mesh=mesh, in_specs=in_specs, out_specs=out_specs, check_vma=False
    )
```

profile of v0, /device:TPU:0, one launch (start us, length us, event | category | flops | bytes accessed | tf_op | source)
XLA Modules:
  0.0 810.7 jit_solution(4811789456164737185)
XLA Ops:
  13.1 6.2 all_gather.27
  19.3 5.4 all_gather.28
  25.4 9.2 %all_gather.30 = bf16[512,512]{1,0:T(8,128)(2,1)} all-gather(bf16[128,512]{1,0:T(8,128)(2,1)S(1)} %copy-done.31), channel_id=1, replica_groups=mesh['expert'=8,'shard'=4] {'shard'}, dimensions={0}, use_global_device_ids=true | all-gather | bytes 655360 | tf_op jit(solution)/shard_map/all_gather | solution.py:64
  68.2 13.4 %scatter_custom_fusion = bf16[3152,512]{1,0:T(8,128)(2,1)} fusion(s32[1576]{0:T(1024)S(1)} %fusion.91, bf16[1576,512]{1,0:T(8,128)(2,1)} %reshape.306, bf16[]{:T(256)} %constant.84.clone.1), kind=kCustom, calls=%fused_computation.86 | custom fusion | bytes 3228160 | tf_op jit(solution)/shard_map/scatter | solution.py:119
  85.2 5.6 all-to-all-start
  92.3 5.2 all_gather.33
  97.5 5.0 all_gather.35
  102.6 13.8 %all-gather.6.cloned.1.call-done = bf16[1,512,2048]{2,1,0:T(8,128)(2,1)} async-done(((bf16[1,512,512]{2,1,0:T(8,128)(2,1)}), bf16[1,512,2048]{2,1,0:T(8,128)(2,1)}) %all-gather.6.cloned.1.call-update) | async-done | bytes 2097168 | tf_op jit(solution)/shard_map/all_gather | solution.py:68
  116.3 48.6 %all-to-all-done = bf16[8,1,394,512]{3,2,1,0:T(8,128)(2,1)} async-done(((bf16[8,1,394,512]{3,2,1,0:T(8,128)(2,1)}), bf16[8,1,394,512]{3,2,1,0:T(8,128)(2,1)}, u32[]{:S(2)}, u32[]{:S(2)}) %all-to-all-start) | async-done | bytes 3227680 | tf_op jit(solution)/shard_map/all_to_all | solution.py:135
  165.0 14.3 %fusion.25 = f32[8,394,2048]{2,1,0:T(8,128)} fusion(bf16[8,1,394,512]{3,2,1,0:T(8,128)(2,1)} %all-to-all-done, bf16[1,512,2048]{2,1,0:T(8,128)(2,1)} %all-gather.6.cloned.1.call-done), kind=kOutput, calls=%fused_computation.44 | convolution fusion | flops 6610223104 | bytes 31145984 | tf_op jit(solution)/shard_map/while/body/eval_jaxpr/sjcd,jdf->sjcf/dot_general | solution.py:125
  179.3 17.0 %fusion.21 = bf16[8,1,394,512]{3,2,1,0:T(8,128)(2,1)} fusion(f32[512]{0:T(512)S(1)} %bitcast.253, bf16[1,2048,512]{2,1,0:T(8,128)(2,1)} %all-gather.8.cloned.1.call-done, f32[8,394,2048]{2,1,0:T(8,128)} %fusion.25, f32[2048]{0:T(1024)S(1)} %bitcast.250), kind=kOutput, calls=%fused_computation.40 | convolution fusion | flops 6678003712 | bytes 31156224 | tf_op jit(solution)/shard_map/while/body/eval_jaxpr/sjcf,jfd->sjcd/dot_general | solution.py:130
  201.5 92.6 %psum.50 = f32[]{:T(128)} all-reduce(f32[]{:T(128)} %convert_reduce_fusion.1), channel_id=1, replica_groups=mesh['expert'=8,'shard'=4] {'expert','shard'}, use_global_device_ids=true, to_apply=%region_18.19 | all-reduce | flops 1 | bytes 8 | tf_op jit(solution)/shard_map/psum | solution.py:148
  294.8 5.6 all_gather.31
  304.4 6.0 gather_fusion
  314.1 17.6 %multiply_reduce_fusion.3 = f32[788,512]{1,0:T(8,128)S(1)} fusion(f32[788,2,512]{2,1,0:T(2,128)S(1)} %reshape.284, f32[788,2]{1,0:T(8,128)} %copy-done.27), kind=kLoop, calls=%fused_computation.49 | loop fusion | flops 1210368 | bytes 4847776 | tf_op jit(solution)/shard_map/reduce_sum | solution.py:144
  336.8 5.3 mul.344
  342.1 18.5 %scatter_custom_fusion.1 = bf16[3152,512]{1,0:T(8,128)(2,1)} fusion(s32[1576]{0:T(1024)S(1)} %fusion.91, f32[1576,512]{1,0:T(8,128)} %mul.344, f32[1576]{0:T(1024)S(1)} %mul.341, bf16[]{:T(256)} %constant.84.clone.1), kind=kCustom, calls=%fused_computation.83 | custom fusion | flops 1613824 | bytes 6463490 | tf_op jit(solution)/shard_map/scatter | solution.py:164
  364.2 79.0 %all_to_all.20 = bf16[8,1,394,512]{3,2,1,0:T(8,128)(2,1)} all-to-all(bf16[8,1,394,512]{3,2,1,0:T(8,128)(2,1)} %bitcast.233), channel_id=1, replica_groups=mesh['expert'=8,'shard'=4] {'expert'}, dimensions={0} | all-to-all | bytes 6455296 | tf_op jit(solution)/shard_map/all_to_all | solution.py:167
  446.5 30.0 %fusion.115 = (bf16[2048]{0:T(1024)(128)(2,1)S(1)}, bf16[8,1,394,2048]{3,2,0,1:T(8,128)(2,1)}) fusion(f32[2048]{0:T(1024)S(1)} %bitcast.251, f32[8,394,2048]{2,1,0:T(8,128)} %fusion.25, bf16[1,2048,512]{2,1,0:T(8,128)(2,1)} %all-gather.8.cloned.1.call-done, bf16[8,1,394,512]{3,2,1,0:T(8,128)(2,1)} %all_to_all.20), kind=kOutput, calls=%fused_computation.173 | convolution fusion | flops 6752237568 | bytes 44068864 | tf_op jit(solution)/shard_map/while/body/eval_jaxpr/sjcd,jfd->sjcf/dot_general | solution.py:182
  477.7 18.2 %fusion.42 = bf16[1,2048,512]{2,1,0:T(8,128)(2,1)} fusion(bf16[8,1,394,512]{3,2,1,0:T(8,128)(2,1)} %all_to_all.20, f32[8,394,2048]{2,1,0:T(8,128)} %fusion.25, f32[2048]{0:T(1024)S(1)} %bitcast.252), kind=kOutput, calls=%fused_computation.52 | convolution fusion | flops 6675824640 | bytes 31154176 | tf_op jit(solution)/shard_map/while/body/eval_jaxpr/sjcf,sjcd->jfd/dot_general | solution.py:178
  496.0 13.6 %convert_bitcast_fusion = bf16[8,1,394,512]{3,2,1,0:T(8,128)(2,1)} fusion(bf16[8,1,394,2048]{3,2,0,1:T(8,128)(2,1)} %get-tuple-element.101, bf16[1,512,2048]{2,1,0:T(8,128)(2,1)} %all-gather.6.cloned.1.call-done), kind=kOutput, calls=%fused_computation.46 | convolution fusion | flops 6611836928 | bytes 18235392 | tf_op jit(solution)/shard_map/while/body/eval_jaxpr/sjcf,jdf->sjcd/dot_general | solution.py:190
  514.1 12.2 %fusion.37 = bf16[1,512,2048]{2,1,0:T(8,128)(2,1)} fusion(bf16[8,1,394,2048]{3,2,0,1:T(8,128)(2,1)} %get-tuple-element.101, bf16[8,1,394,512]{3,2,1,0:T(8,128)(2,1)} %all-to-all-done), kind=kOutput, calls=%fused_computation.51 | convolution fusion | flops 6611271680 | bytes 18235392 | tf_op jit(solution)/shard_map/while/body/eval_jaxpr/sjcd,sjcf->jdf/dot_general | solution.py:187
  538.9 27.8 %reduce-scatter.9.cloned.1.call-done = bf16[1,512,512]{2,1,0:T(8,128)(2,1)} async-done(((bf16[1,512,2048]{2,1,0:T(8,128)(2,1)}), bf16[1,512,512]{2,1,0:T(8,128)(2,1)}) %reduce-scatter.9.cloned.1.call-update) | async-done | bytes 524304 | tf_op jit(solution)/shard_map/reduce_scatter | solution.py:271
  568.8 18.0 %all-to-all-done.3 = bf16[8,1,394,512]{3,2,1,0:T(8,128)(2,1)} async-done(((bf16[8,1,394,512]{3,2,1,0:T(8,128)(2,1)}), bf16[8,1,394,512]{3,2,1,0:T(8,128)(2,1)}, u32[]{:S(2)}, u32[]{:S(2)}) %all-to-all-start.3) | async-done | bytes 3227680 | tf_op jit(solution)/shard_map/all_to_all | solution.py:205
  589.2 6.0 gather_fusion.1
  595.2 4.9 reshape.285
  600.2 7.1 reduce_sum.310
  619.7 7.8 multiply_reduce_fusion
  643.1 7.0 convert_element_type.174
  650.2 5.7 fusion.104
  663.1 39.3 %all-reduce.1 = (f32[]{:T(128)}, f32[512,8]{0,1:T(8,128)S(1)}, f32[2,512]{1,0:T(2,128)S(1)}, f32[2,512]{1,0:T(2,128)S(1)}) all-reduce(f32[]{:T(128)} %get-tuple-element.103, f32[512,8]{0,1:T(8,128)S(1)} %fusion.116, f32[2,512]{1,0:T(2,128)S(1)} %pad_maximum_fusion.1, ...), channel_id=1, replica_groups=mesh['expert'=8,'shard'=4] {'expert','shard'}, use_global_device_ids=true, to_apply=%region_16.17 | all-reduce | flops 6145 | bytes 49160 | tf_op jit(solution)/shard_map/psum | solution.py:148
  708.0 90.6 %all-reduce.5.cloned.1.call-done = (f32[512,1536]{1,0:T(8,128)}, f32[512,512]{1,0:T(8,128)}) async-done(((f32[512,1536]{1,0:T(8,128)}, f32[512,512]{1,0:T(8,128)}), (f32[512,1536]{1,0:T(8,128)}, f32[512,512]{1,0:T(8,128)})) %all-reduce.5.cloned.1.call-update) | async-done | bytes 4194320 | tf_op jit(solution)/shard_map/psum | solution.py:260
  (243 shorter events, 135.3 us)
Async XLA Ops:
  7.2 17.6 %copy-start.9 = (bf16[788,512]{1,0:T(8,128)(2,1)S(1)}, bf16[788,512]{1,0:T(8,128)(2,1)}, u32[]{:S(2)}) copy-start(bf16[788,512]{1,0:T(8,128)(2,1)} %param.13) | copy-start | bytes 2420740
  7.2 18.2 %copy-start.31 = (bf16[128,512]{1,0:T(8,128)(2,1)S(1)}, bf16[128,512]{1,0:T(8,128)(2,1)}, u32[]{:S(2)}) copy-start(bf16[128,512]{1,0:T(8,128)(2,1)} %param.18) | copy-start | bytes 393220
  7.2 27.5 %all-gather.4.cloned.1.call-start = ((), (), s32[]{:S(2)}) async-start(), calls=%async_computation.8 | async-start | bytes 1966080 | tf_op jit(solution)/shard_map/all_gather | solution.py:63
  25.0 12.7 %copy-start.35 = (f32[788]{0:T(1024)}, f32[788]{0:T(1024)S(1)}, u32[]{:S(2)}) copy-start(f32[788]{0:T(1024)S(1)} %broadcast_multiply_fusion.2) | copy-start | bytes 9460
  25.4 9.3 %copy-start.39 = (f32[788]{0:T(1024)}, f32[788]{0:T(1024)S(1)}, u32[]{:S(2)}) copy-start(f32[788]{0:T(1024)S(1)} %fusion.62) | copy-start | bytes 9460
  34.6 30.6 %copy-start.46 = (f32[1,512]{1,0:T(1,128)}, f32[1,512]{1,0:T(1,128)S(1)}, u32[]{:S(2)}) copy-start(f32[1,512]{1,0:T(1,128)S(1)} %get-tuple-element.86) | copy-start | bytes 6148
  65.6 234.9 %copy-start.13 = (bf16[788,512]{1,0:T(8,128)(2,1)}, bf16[788,512]{1,0:T(8,128)(2,1)S(1)}, u32[]{:S(2)}) copy-start(bf16[788,512]{1,0:T(8,128)(2,1)S(1)} %add_convert_fusion) | copy-start | bytes 2420740
  85.2 7.1 copy-start.50
  85.2 12.3 %copy-start.54 = (bf16[1,128]{1,0:T(2,128)(2,1)S(1)}, bf16[1,128]{1,0:T(2,128)(2,1)}, u32[]{:S(2)}) copy-start(bf16[1,128]{1,0:T(2,128)(2,1)} %param.25) | copy-start | bytes 772
  85.2 79.8 %all-to-all-start = ((bf16[8,1,394,512]{3,2,1,0:T(8,128)(2,1)}), bf16[8,1,394,512]{3,2,1,0:T(8,128)(2,1)}, u32[]{:S(2)}, u32[]{:S(2)}) async-start(bf16[8,1,394,512]{3,2,1,0:T(8,128)(2,1)} %bitcast.10), calls=%async_computation | async-start | bytes 6553600 | tf_op jit(solution)/shard_map/all_to_all | solution.py:135
  90.8 25.5 %all-gather.6.cloned.1.call-start = ((), (), s32[]{:S(2)}) async-start(), calls=%async_computation.9 | async-start | bytes 2621440 | tf_op jit(solution)/shard_map/all_gather | solution.py:68
  91.6 87.7 %all-gather.8.cloned.1.call-start = ((), (), s32[]{:S(2)}) async-start(), calls=%async_computation.10 | async-start | bytes 2621440 | tf_op jit(solution)/shard_map/all_gather | solution.py:70
  196.2 98.6 %copy-start.51 = (bf16[128,8]{0,1:T(8,128)(2,1)S(1)}, bf16[128,8]{0,1:T(8,128)(2,1)}, u32[]{:S(2)}) copy-start(bf16[128,8]{0,1:T(8,128)(2,1)} %param.19) | copy-start | bytes 6148
  196.2 104.6 %copy-start.32 = (s32[788,2]{0,1:T(2,128)S(1)}, s32[788,2]{0,1:T(2,128)}, u32[]{:S(2)}) copy-start(s32[788,2]{0,1:T(2,128)} %param.16) | copy-start | bytes 18916
  196.2 105.6 %all-to-all-start.1 = ((bf16[8,1,394,512]{3,2,1,0:T(8,128)(2,1)}), bf16[8,1,394,512]{3,2,1,0:T(8,128)(2,1)}, u32[]{:S(2)}, u32[]{:S(2)}) async-start(bf16[8,1,394,512]{3,2,1,0:T(8,128)(2,1)} %fusion.21), calls=%async_computation.1 | async-start | bytes 6553600 | tf_op jit(solution)/shard_map/all_to_all | solution.py:138
  200.9 332.9 %reduce-scatter.15.cloned.1.call-start = ((), (), s32[]{:S(2)}) async-start(), calls=%async_computation.14 | async-start | bytes 163840
  314.1 17.7 %copy-start.2 = (f32[788,512]{1,0:T(8,128)S(1)}, f32[788,512]{1,0:T(8,128)}, u32[]{:S(2)}) copy-start(f32[788,512]{1,0:T(8,128)} %copy-done.1) | copy-start | bytes 4841476
  314.1 17.7 %copy-start.28 = (bf16[788,512]{1,0:T(8,128)(2,1)S(1)}, bf16[788,512]{1,0:T(8,128)(2,1)}, u32[]{:S(2)}) copy-start(bf16[788,512]{1,0:T(8,128)(2,1)} %param.14) | copy-start | bytes 2420740
  446.4 88.7 %reduce-scatter.13.cloned.1.call-start = ((), (), s32[]{:S(2)}) async-start(), calls=%async_computation.13 | async-start | bytes 655360
  477.7 59.1 %reduce-scatter.11.cloned.1.call-start = ((), (), s32[]{:S(2)}) async-start(), calls=%async_computation.12 | async-start | bytes 2621440 | tf_op jit(solution)/shard_map/reduce_scatter | solution.py:277
  509.6 77.3 %all-to-all-start.3 = ((bf16[8,1,394,512]{3,2,1,0:T(8,128)(2,1)}), bf16[8,1,394,512]{3,2,1,0:T(8,128)(2,1)}, u32[]{:S(2)}, u32[]{:S(2)}) async-start(bf16[8,1,394,512]{3,2,1,0:T(8,128)(2,1)} %convert_bitcast_fusion), calls=%async_computation.3 | async-start | bytes 6553600 | tf_op jit(solution)/shard_map/all_to_all | solution.py:205
  514.0 52.6 %reduce-scatter.9.cloned.1.call-start = ((), (), s32[]{:S(2)}) async-start(), calls=%async_computation.11 | async-start | bytes 2621440 | tf_op jit(solution)/shard_map/reduce_scatter | solution.py:271
  526.3 272.2 %all-reduce.5.cloned.1.call-start = ((), (), s32[]{:S(2)}) async-start(), calls=%async_computation.15 | async-start | bytes 8388608 | tf_op jit(solution)/shard_map/psum | solution.py:260
  600.2 7.1 copy-start.3
  600.2 7.1 copy-start.12
  600.2 7.1 copy-start.34
  600.2 7.1 copy-start.38
  600.2 7.1 copy-start.47
  616.5 11.0 %slice-start = ((s8[6553600]{0:T(1024)(128)(4,1)}), s8[2359296]{0:T(1024)(128)(4,1)S(1)}, s32[]{:S(2)}) async-start(s8[6553600]{0:T(1024)(128)(4,1)} %bitcast.231), calls=%async_computation.16 | async-start | bytes 4718592
  619.7 7.8 slice-start.1
  643.1 7.1 copy-start.53
  661.1 43.8 %copy-start.8 = (f32[788,512]{1,0:T(8,128)S(1)}, f32[788,512]{1,0:T(8,128)}, u32[]{:S(2)}) copy-start(f32[788,512]{1,0:T(8,128)} %copy-done.6) | copy-start | bytes 4841476
  (37 other events, 108.2 us)
Sparse Core Ops, SparseCore 0:
  9.6 23.7 all-gather.3
  93.2 23.0 all-gather.5
  117.9 22.5 all-gather.7
  446.6 18.7 reduce-scatter.14
  477.8 20.7 reduce-scatter.12
  501.0 31.4 reduce-scatter.10
  535.2 31.4 reduce-scatter.8
  656.1 142.4 all-reduce.4
where the time goes:
time: 818 us; the launch traced here: 811 us
  blocking collectives  248 us (30%)
  waiting for transfers between devices  201 us (25%)
  matrix products  143 us (17%)
  local copies, waits for them, and re-layouts  113 us (14%)
  other arithmetic  72.9 us (9%)
  between operations  18.7 us (2%)
  starting transfers between devices  15.2 us (2%)
    psum x2, blocking collectives, per_device(): lax.psum((squared_sum, jnp.sum(valid_rows)), ('expert', 'shard'))  132 us
    psum x1, waiting for transfers between devices, per_device(): lax.psum((mixer_term, merge_term, router_term, gain_term, shift_term), ('...  90.6 us
    all_to_all x1, blocking collectives, per_device(): lax.all_to_all(grad_send, 'expert', split_axis=0, concat_axis=0, tiled=True)  79 us
    all_to_all x1, waiting for transfers between devices, per_device(): lax.all_to_all(send_rows, 'expert', split_axis=0, concat_axis=0, tiled=True)  48.6 us
    dot_general x1, matrix products, expert_backward(): jnp.einsum('sjcd,jfd->sjcf', grads_block, down_full, preferred_element_ty...  30 us
    reduce_scatter x1, waiting for transfers between devices, per_device(): lax.psum_scatter(up_total.astype(jnp.bfloat16), 'shard', scatter_dimensio...  27.8 us
    unnamed x125, local copies, waits for them, and re-layouts  19.9 us
    scatter x1, other arithmetic, per_device(): jnp.zeros((experts * capacity, model_width), jnp.bfloat16).at[slot_rows]  18.5 us
  transfers between devices with their start and end apart: 11, of which 5 were waited for; matrix products, arithmetic and copies ran while one was open for 15% of the time, Pallas kernels for 0%

commit v1 on v0

--- a/solution.py
+++ b/solution.py
@@ -7,6 +7,11 @@
 HEAD_DIM = 64
 SEQ = 197
 norm_eps = 1e-06
+
+
+def one_after_other(array, axis_one, axis_two):
+    half = lax.psum(array, axis_one)
+    return lax.psum(half, axis_two)
 
 
 def layer_norm(inputs, scale_row, shift_row):
@@ -145,7 +150,9 @@
     valid_rows = valid_mask.astype(jnp.float32)
     error_rows = block_out - teacher.astype(jnp.float32)
     squared_sum = jnp.sum(valid_rows * jnp.sum(error_rows * error_rows, axis=1))
-    total_error, total_count = lax.psum((squared_sum, jnp.sum(valid_rows)), ("expert", "shard"))
+    total_error, total_count = one_after_other(
+        (squared_sum, jnp.sum(valid_rows)), "shard", "expert"
+    )
     loss_value = total_error / (2.0 * total_count)
     all_tokens = token_count * expert_ways * shard_ways
     final_grad = all_tokens / total_count * valid_rows[:, None] * error_rows

time: 818 us -> 775 us (0.947)
  waiting for transfers between devices: 201 us -> 151 us
  blocking collectives: 248 us -> 260 us
  matrix products: 143 us -> 133 us
    psum x1, waiting for transfers between devices: 90.6 us -> 59.8 us  [per_device(): lax.psum((mixer_term, merge_term, router_term, gain_term, shift_term), ('...]
    reduce_scatter x1, waiting for transfers between devices: 27.8 us -> 0.01 us  [per_device(): lax.psum_scatter(up_total.astype(jnp.bfloat16), 'shard', scatter_dimensio...]
    all_to_all x1, blocking collectives: 79 us -> 91 us  [per_device(): lax.all_to_all(grad_send, 'expert', split_axis=0, concat_axis=0, tiled=True)]
    unnamed x125 -> x133, local copies, waits for them, and re-layouts: 19.9 us -> 24.8 us
    psum x2 -> x5, blocking collectives: 132 us -> 133 us  [the longest x2 82.1 us: one_after_other(): return lax.psum(half, axis_two)]
  transfers between devices with their start and end apart: 11 -> 11, of which waited for: 5 -> 5; matrix products, arithmetic and copies ran while one was open for 15% -> 19% of each run, Pallas kernels for 0% -> 0%
where the time goes in v1:
time: 775 us; the launch traced here: 768 us
  blocking collectives  260 us (34%)
  waiting for transfers between devices  151 us (19%)
  matrix products  133 us (17%)
  local copies, waits for them, and re-layouts  117 us (15%)
  other arithmetic  72.9 us (9%)
  between operations  18.5 us (2%)
  starting transfers between devices  15.7 us (2%)
    all_to_all x1, blocking collectives, per_device(): lax.all_to_all(grad_send, 'expert', split_axis=0, concat_axis=0, tiled=True)  91 us
    psum x2, blocking collectives, one_after_other(): return lax.psum(half, axis_two)  82.1 us
    psum x1, waiting for transfers between devices, per_device(): lax.psum((mixer_term, merge_term, router_term, gain_term, shift_term), ('...  59.8 us
    all_to_all x1, waiting for transfers between devices, per_device(): lax.all_to_all(send_rows, 'expert', split_axis=0, concat_axis=0, tiled=True)  48.6 us
    psum x1, blocking collectives, per_device(): lax.psum((mixer_term, merge_term, router_term, gain_term, shift_term), ('...  37.3 us
    dot_general x1, matrix products, expert_backward(): jnp.einsum('sjcd,jfd->sjcf', grads_block, down_full, preferred_element_ty...  25.6 us
    unnamed x133, local copies, waits for them, and re-layouts  24.8 us
    all_to_all x1, waiting for transfers between devices, per_device(): lax.all_to_all(input_grads.reshape(arrived.shape), 'expert', split_axis=0...  22.8 us
  transfers between devices with their start and end apart: 11, of which 5 were waited for; matrix products, arithmetic and copies ran while one was open for 19% of the time, Pallas kernels for 0%

profile of v1, /device:TPU:0, one launch (start us, length us, event | category | flops | bytes accessed | tf_op | source)
XLA Modules:
  0.0 767.7 jit_solution(7873603987749610147)
XLA Ops:
  13.1 6.2 all_gather.27
  19.3 5.4 all_gather.28
  25.4 9.2 %all_gather.30 = bf16[512,512]{1,0:T(8,128)(2,1)} all-gather(bf16[128,512]{1,0:T(8,128)(2,1)S(1)} %copy-done.32), channel_id=1, replica_groups=mesh['expert'=8,'shard'=4] {'shard'}, dimensions={0}, use_global_device_ids=true | all-gather | bytes 655360 | tf_op jit(solution)/shard_map/all_gather | solution.py:69
  68.2 13.2 %scatter_custom_fusion = bf16[3152,512]{1,0:T(8,128)(2,1)} fusion(s32[1576]{0:T(1024)S(1)} %fusion.91, bf16[1576,512]{1,0:T(8,128)(2,1)} %reshape.306, bf16[]{:T(256)} %constant.84.clone.1), kind=kCustom, calls=%fused_computation.86 | custom fusion | bytes 3228160 | tf_op jit(solution)/shard_map/scatter | solution.py:124
  85.0 5.7 all-to-all-start
  92.2 5.2 all_gather.33
  97.4 5.0 all_gather.35
  102.4 13.8 %all-gather.6.cloned.1.call-done = bf16[1,512,2048]{2,1,0:T(8,128)(2,1)} async-done(((bf16[1,512,512]{2,1,0:T(8,128)(2,1)}), bf16[1,512,2048]{2,1,0:T(8,128)(2,1)}) %all-gather.6.cloned.1.call-update) | async-done | bytes 2097168 | tf_op jit(solution)/shard_map/all_gather | solution.py:73
  116.2 48.6 %all-to-all-done = bf16[8,1,394,512]{3,2,1,0:T(8,128)(2,1)} async-done(((bf16[8,1,394,512]{3,2,1,0:T(8,128)(2,1)}), bf16[8,1,394,512]{3,2,1,0:T(8,128)(2,1)}, u32[]{:S(2)}, u32[]{:S(2)}) %all-to-all-start) | async-done | bytes 3227680 | tf_op jit(solution)/shard_map/all_to_all | solution.py:140
  164.8 14.3 %fusion.25 = f32[8,394,2048]{2,1,0:T(8,128)} fusion(bf16[8,1,394,512]{3,2,1,0:T(8,128)(2,1)} %all-to-all-done, bf16[1,512,2048]{2,1,0:T(8,128)(2,1)} %all-gather.6.cloned.1.call-done), kind=kOutput, calls=%fused_computation.44 | convolution fusion | flops 6610223104 | bytes 31145984 | tf_op jit(solution)/shard_map/while/body/eval_jaxpr/sjcd,jdf->sjcf/dot_general | solution.py:130
  179.1 16.9 %fusion.21 = bf16[8,1,394,512]{3,2,1,0:T(8,128)(2,1)} fusion(f32[512]{0:T(512)S(1)} %bitcast.253, bf16[1,2048,512]{2,1,0:T(8,128)(2,1)} %all-gather.8.cloned.1.call-done, f32[8,394,2048]{2,1,0:T(8,128)} %fusion.25, f32[2048]{0:T(1024)S(1)} %bitcast.250), kind=kOutput, calls=%fused_computation.40 | convolution fusion | flops 6678003712 | bytes 31156224 | tf_op jit(solution)/shard_map/while/body/eval_jaxpr/sjcf,jfd->sjcd/dot_general | solution.py:135
  201.3 6.7 psum.65
  208.0 61.8 %psum.66 = f32[]{:T(128)} all-reduce(f32[]{:T(128)} %psum.65), channel_id=1, replica_groups=mesh['expert'=8,'shard'=4] {'expert'}, use_global_device_ids=true, to_apply=%region_20.21 | all-reduce | flops 1 | bytes 8 | tf_op jit(solution)/shard_map/psum | solution.py:14
  270.5 5.2 all_gather.31
  279.8 6.1 gather_fusion
  289.5 17.6 %multiply_reduce_fusion.3 = f32[788,512]{1,0:T(8,128)S(1)} fusion(f32[788,2,512]{2,1,0:T(2,128)S(1)} %reshape.284, f32[788,2]{1,0:T(8,128)} %copy-done.27), kind=kLoop, calls=%fused_computation.49 | loop fusion | flops 1210368 | bytes 4847776 | tf_op jit(solution)/shard_map/reduce_sum | solution.py:149
  312.3 5.3 mul.344
  317.6 18.4 %scatter_custom_fusion.1 = bf16[3152,512]{1,0:T(8,128)(2,1)} fusion(s32[1576]{0:T(1024)S(1)} %fusion.91, f32[1576,512]{1,0:T(8,128)} %mul.344, f32[1576]{0:T(1024)S(1)} %mul.341, bf16[]{:T(256)} %constant.84.clone.1), kind=kCustom, calls=%fused_computation.83 | custom fusion | flops 1613824 | bytes 6463490 | tf_op jit(solution)/shard_map/scatter | solution.py:171
  339.6 91.0 %all_to_all.20 = bf16[8,1,394,512]{3,2,1,0:T(8,128)(2,1)S(1)} all-to-all(bf16[8,1,394,512]{3,2,1,0:T(8,128)(2,1)} %bitcast.233), channel_id=1, replica_groups=mesh['expert'=8,'shard'=4] {'expert'}, dimensions={0} | all-to-all | bytes 6455296 | tf_op jit(solution)/shard_map/all_to_all | solution.py:174
  430.6 25.6 %fusion.115 = (bf16[2048]{0:T(1024)(128)(2,1)S(1)}, bf16[8,1,394,2048]{3,2,0,1:T(8,128)(2,1)S(1)}) fusion(f32[2048]{0:T(1024)S(1)} %bitcast.251, f32[8,394,2048]{2,1,0:T(8,128)} %fusion.25, bf16[1,2048,512]{2,1,0:T(8,128)(2,1)S(1)} %copy-done.58, bf16[8,1,394,512]{3,2,1,0:T(8,128)(2,1)S(1)} %all_to_all.20), kind=kOutput, calls=%fused_computation.173 | convolution fusion | flops 6752237568 | bytes 44068864 | tf_op jit(solution)/shard_map/while/body/eval_jaxpr/sjcd,jfd->sjcf/dot_general | solution.py:189
  461.0 8.8 %convert_bitcast_fusion = bf16[8,1,394,512]{3,2,1,0:T(8,128)(2,1)} fusion(bf16[8,1,394,2048]{3,2,0,1:T(8,128)(2,1)S(1)} %get-tuple-element.100, bf16[1,512,2048]{2,1,0:T(8,128)(2,1)S(1)} %copy-done.57), kind=kOutput, calls=%fused_computation.46 | convolution fusion | flops 6611836928 | bytes 18235392 | tf_op jit(solution)/shard_map/while/body/eval_jaxpr/sjcf,jdf->sjcd/dot_general | solution.py:197
  479.0 18.3 %fusion.42 = bf16[1,2048,512]{2,1,0:T(8,128)(2,1)} fusion(bf16[8,1,394,512]{3,2,1,0:T(8,128)(2,1)} %copy-done.12, f32[8,394,2048]{2,1,0:T(8,128)} %fusion.25, f32[2048]{0:T(1024)S(1)} %bitcast.252), kind=kOutput, calls=%fused_computation.52 | convolution fusion | flops 6675824640 | bytes 31154176 | tf_op jit(solution)/shard_map/while/body/eval_jaxpr/sjcf,sjcd->jfd/dot_general | solution.py:185
  504.6 12.4 %fusion.37 = bf16[1,512,2048]{2,1,0:T(8,128)(2,1)} fusion(bf16[8,1,394,2048]{3,2,0,1:T(8,128)(2,1)} %copy-done.59, bf16[8,1,394,512]{3,2,1,0:T(8,128)(2,1)} %all-to-all-done), kind=kOutput, calls=%fused_computation.51 | convolution fusion | flops 6611271680 | bytes 18235392 | tf_op jit(solution)/shard_map/while/body/eval_jaxpr/sjcd,sjcf->jdf/dot_general | solution.py:194
  524.2 22.8 %all-to-all-done.3 = bf16[8,1,394,512]{3,2,1,0:T(8,128)(2,1)} async-done(((bf16[8,1,394,512]{3,2,1,0:T(8,128)(2,1)}), bf16[8,1,394,512]{3,2,1,0:T(8,128)(2,1)}, u32[]{:S(2)}, u32[]{:S(2)}) %all-to-all-start.3) | async-done | bytes 3227680 | tf_op jit(solution)/shard_map/all_to_all | solution.py:212
  549.4 6.0 gather_fusion.1
  560.4 7.1 reduce_sum.310
  580.0 7.8 %multiply_reduce_fusion = (f32[4,8,197]{2,1,0:T(8,128)S(1)}, f32[4,8,197,197]{2,3,1,0:T(8,128)}) fusion(f32[4,8,197,197]{2,3,1,0:T(8,128)} %copy-done, f32[4,8,197]{2,1,0:T(8,128)S(1)} %copy-done.31, bf16[4,197,8,64]{1,3,2,0:T(8,128)(2,1)} %copy.115, bf16[4,197,1,8,64]{1,4,3,0,2:T(8,128)(2,1)S(1)} %copy-done.19), kind=kOutput, calls=%fused_computation.32 | convolution fusion | flops 163922912 | bytes 11599360 | tf_op jit(solution)/shard_map/bqhd,bkhd->bhqk/dot_general | solution.py:241
  601.3 7.1 convert_element_type.174
  618.2 6.7 psum.63
  627.1 20.3 %psum.64 = f32[]{:T(128)} all-reduce(f32[]{:T(128)} %psum.63), channel_id=1, replica_groups=mesh['expert'=8,'shard'=4] {'expert'}, use_global_device_ids=true, to_apply=%region_17.18 | all-reduce | flops 1 | bytes 8 | tf_op jit(solution)/shard_map/psum | solution.py:14
  654.3 37.3 %all-reduce.1 = (f32[512,8]{0,1:T(8,128)S(1)}, f32[2,512]{1,0:T(2,128)S(1)}, f32[2,512]{1,0:T(2,128)S(1)}) all-reduce(f32[512,8]{0,1:T(8,128)S(1)} %fusion.116, f32[2,512]{1,0:T(2,128)S(1)} %pad_maximum_fusion.1, f32[2,512]{1,0:T(2,128)S(1)} %pad_maximum_fusion.2), channel_id=1, replica_groups=mesh['expert'=8,'shard'=4] {'expert','shard'}, use_global_device_ids=true, to_apply=%region_33.34 | all-reduce | flops 6144 | bytes 49152 | tf_op jit(solution)/shard_map/psum | solution.py:267
  696.0 59.8 %all-reduce.5.cloned.1.call-done = (f32[512,1536]{1,0:T(8,128)}, f32[512,512]{1,0:T(8,128)}) async-done(((f32[512,1536]{1,0:T(8,128)}, f32[512,512]{1,0:T(8,128)}), (f32[512,1536]{1,0:T(8,128)}, f32[512,512]{1,0:T(8,128)})) %all-reduce.5.cloned.1.call-update) | async-done | bytes 4194320 | tf_op jit(solution)/shard_map/psum | solution.py:267
  (254 shorter events, 153.5 us)
Async XLA Ops:
  7.2 17.6 %copy-start.8 = (bf16[788,512]{1,0:T(8,128)(2,1)S(1)}, bf16[788,512]{1,0:T(8,128)(2,1)}, u32[]{:S(2)}) copy-start(bf16[788,512]{1,0:T(8,128)(2,1)} %param.13) | copy-start | bytes 2420740
  7.2 18.2 %copy-start.32 = (bf16[128,512]{1,0:T(8,128)(2,1)S(1)}, bf16[128,512]{1,0:T(8,128)(2,1)}, u32[]{:S(2)}) copy-start(bf16[128,512]{1,0:T(8,128)(2,1)} %param.18) | copy-start | bytes 393220
  7.2 27.5 %all-gather.4.cloned.1.call-start = ((), (), s32[]{:S(2)}) async-start(), calls=%async_computation.8 | async-start | bytes 1966080 | tf_op jit(solution)/shard_map/all_gather | solution.py:68
  25.0 12.7 %copy-start.36 = (f32[788]{0:T(1024)}, f32[788]{0:T(1024)S(1)}, u32[]{:S(2)}) copy-start(f32[788]{0:T(1024)S(1)} %broadcast_multiply_fusion.2) | copy-start | bytes 9460
  25.4 9.3 %copy-start.40 = (f32[788]{0:T(1024)}, f32[788]{0:T(1024)S(1)}, u32[]{:S(2)}) copy-start(f32[788]{0:T(1024)S(1)} %fusion.62) | copy-start | bytes 9460
  34.6 30.5 %copy-start.48 = (f32[1,512]{1,0:T(1,128)}, f32[1,512]{1,0:T(1,128)S(1)}, u32[]{:S(2)}) copy-start(f32[1,512]{1,0:T(1,128)S(1)} %get-tuple-element.85) | copy-start | bytes 6148
  65.6 210.0 %copy-start.13 = (bf16[788,512]{1,0:T(8,128)(2,1)}, bf16[788,512]{1,0:T(8,128)(2,1)S(1)}, u32[]{:S(2)}) copy-start(bf16[788,512]{1,0:T(8,128)(2,1)S(1)} %add_convert_fusion) | copy-start | bytes 2420740
  85.0 7.1 copy-start.52
  85.0 12.3 %copy-start.56 = (bf16[1,128]{1,0:T(2,128)(2,1)S(1)}, bf16[1,128]{1,0:T(2,128)(2,1)}, u32[]{:S(2)}) copy-start(bf16[1,128]{1,0:T(2,128)(2,1)} %param.25) | copy-start | bytes 772
  85.0 79.8 %all-to-all-start = ((bf16[8,1,394,512]{3,2,1,0:T(8,128)(2,1)}), bf16[8,1,394,512]{3,2,1,0:T(8,128)(2,1)}, u32[]{:S(2)}, u32[]{:S(2)}) async-start(bf16[8,1,394,512]{3,2,1,0:T(8,128)(2,1)} %bitcast.10), calls=%async_computation | async-start | bytes 6553600 | tf_op jit(solution)/shard_map/all_to_all | solution.py:140
  90.7 25.5 %all-gather.6.cloned.1.call-start = ((), (), s32[]{:S(2)}) async-start(), calls=%async_computation.9 | async-start | bytes 2621440 | tf_op jit(solution)/shard_map/all_gather | solution.py:73
  91.4 87.7 %all-gather.8.cloned.1.call-start = ((), (), s32[]{:S(2)}) async-start(), calls=%async_computation.10 | async-start | bytes 2621440 | tf_op jit(solution)/shard_map/all_gather | solution.py:75
  196.1 74.4 %copy-start.53 = (bf16[128,8]{0,1:T(8,128)(2,1)S(1)}, bf16[128,8]{0,1:T(8,128)(2,1)}, u32[]{:S(2)}) copy-start(bf16[128,8]{0,1:T(8,128)(2,1)} %param.19) | copy-start | bytes 6148
  196.1 80.0 %copy-start.33 = (s32[788,2]{0,1:T(2,128)S(1)}, s32[788,2]{0,1:T(2,128)}, u32[]{:S(2)}) copy-start(s32[788,2]{0,1:T(2,128)} %param.16) | copy-start | bytes 18916
  196.1 81.0 %all-to-all-start.1 = ((bf16[8,1,394,512]{3,2,1,0:T(8,128)(2,1)}), bf16[8,1,394,512]{3,2,1,0:T(8,128)(2,1)}, u32[]{:S(2)}, u32[]{:S(2)}) async-start(bf16[8,1,394,512]{3,2,1,0:T(8,128)(2,1)} %fusion.21), calls=%async_computation.1 | async-start | bytes 6553600 | tf_op jit(solution)/shard_map/all_to_all | solution.py:143
  289.5 17.7 %copy-start.2 = (f32[788,512]{1,0:T(8,128)S(1)}, f32[788,512]{1,0:T(8,128)}, u32[]{:S(2)}) copy-start(f32[788,512]{1,0:T(8,128)} %copy-done.1) | copy-start | bytes 4841476
  289.5 17.7 %copy-start.28 = (bf16[788,512]{1,0:T(8,128)(2,1)S(1)}, bf16[788,512]{1,0:T(8,128)(2,1)}, u32[]{:S(2)}) copy-start(bf16[788,512]{1,0:T(8,128)(2,1)} %param.14) | copy-start | bytes 2420740
  339.6 91.0 %copy-start.58 = (bf16[1,2048,512]{2,1,0:T(8,128)(2,1)S(1)}, bf16[1,2048,512]{2,1,0:T(8,128)(2,1)}, u32[]{:S(2)}) copy-start(bf16[1,2048,512]{2,1,0:T(8,128)(2,1)} %all-gather.8.cloned.1.call-done) | copy-start | bytes 6291460
  430.6 25.7 %copy-start.12 = (bf16[8,1,394,512]{3,2,1,0:T(8,128)(2,1)}, bf16[8,1,394,512]{3,2,1,0:T(8,128)(2,1)S(1)}, u32[]{:S(2)}) copy-start(bf16[8,1,394,512]{3,2,1,0:T(8,128)(2,1)S(1)} %all_to_all.20) | copy-start | bytes 9682948
  430.6 30.4 %copy-start.57 = (bf16[1,512,2048]{2,1,0:T(8,128)(2,1)S(1)}, bf16[1,512,2048]{2,1,0:T(8,128)(2,1)}, u32[]{:S(2)}) copy-start(bf16[1,512,2048]{2,1,0:T(8,128)(2,1)} %all-gather.6.cloned.1.call-done) | copy-start | bytes 6291460
  469.8 77.2 %all-to-all-start.3 = ((bf16[8,1,394,512]{3,2,1,0:T(8,128)(2,1)}), bf16[8,1,394,512]{3,2,1,0:T(8,128)(2,1)}, u32[]{:S(2)}, u32[]{:S(2)}) async-start(bf16[8,1,394,512]{3,2,1,0:T(8,128)(2,1)} %convert_bitcast_fusion), calls=%async_computation.3 | async-start | bytes 6553600 | tf_op jit(solution)/shard_map/all_to_all | solution.py:212
  474.2 43.3 %reduce-scatter.15.cloned.1.call-start = ((), (), s32[]{:S(2)}) async-start(), calls=%async_computation.14 | async-start | bytes 163840
  477.8 44.9 %reduce-scatter.13.cloned.1.call-start = ((), (), s32[]{:S(2)}) async-start(), calls=%async_computation.13 | async-start | bytes 655360
  479.0 137.1 %reduce-scatter.11.cloned.1.call-start = ((), (), s32[]{:S(2)}) async-start(), calls=%async_computation.12 | async-start | bytes 2621440 | tf_op jit(solution)/shard_map/reduce_scatter | solution.py:284
  497.3 127.6 %reduce-scatter.9.cloned.1.call-start = ((), (), s32[]{:S(2)}) async-start(), calls=%async_computation.11 | async-start | bytes 2621440 | tf_op jit(solution)/shard_map/reduce_scatter | solution.py:278
  517.1 238.7 %all-reduce.5.cloned.1.call-start = ((), (), s32[]{:S(2)}) async-start(), calls=%async_computation.15 | async-start | bytes 8388608 | tf_op jit(solution)/shard_map/psum | solution.py:267
  560.4 7.1 copy-start.3
  560.4 7.1 copy-start.11
  560.4 7.1 copy-start.35
  560.4 7.1 copy-start.39
  576.9 11.0 %slice-start = ((s8[6553600]{0:T(1024)(128)(4,1)}), s8[2359296]{0:T(1024)(128)(4,1)S(1)}, s32[]{:S(2)}) async-start(s8[6553600]{0:T(1024)(128)(4,1)} %bitcast.231), calls=%async_computation.16 | async-start | bytes 4718592
  580.0 7.8 %slice-start.1 = ((s8[6553600]{0:T(1024)(128)(4,1)}), s8[4194304]{0:T(1024)(128)(4,1)S(1)}, s32[]{:S(2)}) async-start(s8[6553600]{0:T(1024)(128)(4,1)} %bitcast.231), calls=%async_computation.17 | async-start | bytes 8388608
  (41 other events, 117.1 us)
Sparse Core Ops, SparseCore 0:
  9.6 23.7 all-gather.3
  93.1 23.0 all-gather.5
  117.7 22.5 all-gather.7
  477.9 19.9 reduce-scatter.14
  500.9 21.6 reduce-scatter.12
  525.0 31.4 reduce-scatter.10
  559.1 31.3 reduce-scatter.8
  614.9 140.7 all-reduce.4
